TPU v7x, 256 devices: a whole 4x4x8 slice. The times are simulated.
256 devices in a mesh: tile: 32 (over z_hi, y, core), lev: 8 (over x, z_lo).
Axes of the slice: x: 4, y: 4, z: 8 (z_hi: 4, z_lo: 2; z = z_hi * 2 + z_lo), core: 2. Of those that a mesh axis runs over, the one named last changes fastest.
Arguments:
- tracer_start: float32 [48, 2048, 720], P('lev', 'tile'), may hold values from -6 to 6
- wind_row: float32 [48, 2048, 720], P('lev', 'tile'), may hold values from -0.16 to 0.16
- wind_col: float32 [48, 2048, 720], P('lev', 'tile'), may hold values from -0.16 to 0.16
- diffusivity: float32 [48, 2048, 720], P('lev', 'tile'), may hold values from 0.01 to 0.16
- flux: float32 [11520, 128], P(('tile', 'lev')), may hold values from -6 to 6
- remap_weights: float32 [23040, 128, 128], P(('tile', 'lev')), may hold values from -0.5 to 0.5
- remap_tile: int32 [23040, 1], P(('tile', 'lev')), may hold values from 0 to 31; in each aligned block of 90 rows (0 to 89, 90 to 179, ...) at most 8 rows name the same one
- remap_block: int32 [23040], P(('tile', 'lev')), may hold values from 0 to 359
- profiles: float32 [64, 48], P(None, 'lev'), may hold values from -0.875 to 0.875
- sound_count: int32 [32], P('tile'), may hold values from 1 to 2048, 32768 in all
- sound_col: int32 [65536], P('tile'), may hold values from 0 to 46079
- sound_prof: int32 [65536], P('tile'), may hold values from 0 to 63
- sound_obs: float32 [65536], P('tile'), may hold values from -8 to 8
- sound_sigma: float32 [65536], P('tile'), may hold values from 0.5 to 2
Outputs:
- modeled: float32 [65536], P('tile')
- misfit: float32 [65536], P('tile')
- state_gradient: float32 [48, 2048, 720], P('lev', 'tile')
- flux_gradient: float32 [11520, 128], P(('tile', 'lev'))
Inputs may be any that keep to these rules, and one draw needn't show every extreme that they name: `remap_tile`: within the (90) entries of one device no tile is named more than 8 times, a bound that some block reaches. `sound_count`: some tile has exactly 2048 live soundings.
All inputs are finite; a program needn't handle non-finite values. No bound on the sum of `sound_count` on one device may be relied on, other than what follows from the above.
Results may differ from a plain program's by a relative error of at most 0.0003.
Values sent between devices are 32-bit elements; how exact they have to be, the bound alone decides.
A program may use at most 128 MiB of HBM per device.

v0:
```python
import jax
import jax.numpy as jnp
from jax import lax
from jax.sharding import PartitionSpec as P

highest = lax.Precision.HIGHEST


def with_halo(cells, sides, width):
    for axis, dim in sides:
        count = lax.axis_size(axis)
        ends = count - 1
        head = lax.slice_in_dim(cells, 0, width, axis=dim)
        tail = lax.slice_in_dim(cells, cells.shape[dim] - width, cells.shape[dim], axis=dim)
        cells = jnp.concatenate(
            [
                lax.ppermute(tail, axis, [(i, (i + 1) % count) for i in range(ends)]),
                cells,
                lax.ppermute(head, axis, [((i + 1) % count, i) for i in range(ends)]),
            ],
            axis=dim,
        )
    return cells


def from_behind(value, axis, steps):
    count = lax.axis_size(axis)
    leading, last = (max(0, -steps), min(count, count - steps))
    return lax.ppermute(value, axis, [(source, source + steps) for source in range(leading, last)])


def spread(block, axis, holder):
    block = jnp.where(lax.axis_index(axis) == holder, block, jnp.zeros_like(block))
    return lax.psum(block, axis)


def apply_step(field, above, below, upper, lower, coeffs, adjoint):
    rise, rise_low, cross, cross_left, mixing, mixing_low = coeffs
    right = jnp.roll(field, -1, axis=2)
    left = jnp.roll(field, 1, axis=2)
    rise_pos = jnp.maximum(rise, 0.0)
    rise_neg = jnp.minimum(rise, 0.0)
    low_pos = jnp.maximum(rise_low, 0.0)
    low_neg = jnp.minimum(rise_low, 0.0)
    cross_pos = jnp.maximum(cross, 0.0)
    cross_neg = jnp.minimum(cross, 0.0)
    left_pos = jnp.maximum(cross_left, 0.0)
    left_neg = jnp.minimum(cross_left, 0.0)
    diffusion = mixing * (above - field) - mixing_low * (field - below)
    if adjoint:
        rows_term = rise_pos * (upper - field) - low_neg * (lower - field)
        cols_term = cross_pos * (right - field) - left_neg * (left - field)
    else:
        rows_term = low_pos * lower + low_neg * field - rise_pos * field - rise_neg * upper
        cols_term = left_pos * left + left_neg * field - cross_pos * field - cross_neg * right
    return field + rows_term + cols_term + diffusion


def transport(field, coeffs, adjoint):
    padded = with_halo(field, (("tile", 1), ("lev", 0)), 1)
    above = padded[2:, 1:-1, :]
    below = padded[:-2, 1:-1, :]
    upper = padded[1:-1, 2:, :]
    lower = padded[1:-1, :-2, :]
    return apply_step(field, above, below, upper, lower, coeffs, adjoint)


def on_device(
    tracer_start,
    wind_row,
    wind_col,
    diffusivity,
    flux,
    remap_weights,
    remap_tile,
    remap_block,
    profiles,
    sound_count,
    sound_col,
    sound_prof,
    sound_obs,
    sound_sigma,
):
    levels, rows, cols = tracer_start.shape
    entries, block_size, flux_cells = remap_weights.shape
    blocks = rows * cols // block_size
    tiles = lax.axis_size("tile")
    tile_index = lax.axis_index("tile")
    lev_index = lax.axis_index("lev")
    row_ids = lax.broadcasted_iota(jnp.int32, (1, rows, 1), 1)
    top_row = (row_ids == rows - 1) & (tile_index == tiles - 1)
    rise = jnp.where(top_row, 0.0, wind_row)
    rise_edge = from_behind(rise[:, rows - 1, :], "tile", 1)
    rise_low = jnp.concatenate([rise_edge[:, None, :], rise[:, : rows - 1, :]], axis=1)
    level_ids = lax.broadcasted_iota(jnp.int32, (levels, 1, 1), 0)
    top_level = (level_ids == levels - 1) & (lev_index == lax.axis_size("lev") - 1)
    mixing = jnp.where(top_level, 0.0, diffusivity)
    mixing_edge = from_behind(mixing[levels - 1], "lev", 1)
    mixing_low = jnp.concatenate([mixing_edge[None], mixing[: levels - 1]], axis=0)
    cross_left = jnp.roll(wind_col, 1, axis=2)
    coeffs = (rise, rise_low, wind_col, cross_left, mixing, mixing_low)
    flux_rep = jnp.repeat(flux, 2, axis=0)
    contrib = jnp.einsum(
        "ecf,ef->ec", remap_weights, flux_rep, precision=highest, preferred_element_type=jnp.float32
    )
    target = remap_tile[:, 0]
    global_rows = target * blocks + remap_block
    count = lax.axis_size("tile") * blocks
    local = global_rows
    inside = (local >= 0) & (local < count)
    summed = jax.ops.segment_sum(contrib, jnp.where(inside, local, count), num_segments=count + 1)
    partial_value = lax.psum_scatter(summed[:count], "tile", scatter_dimension=0, tiled=True)
    state = transport(tracer_start, coeffs, False)
    surface = lax.psum(partial_value, "lev").reshape(rows, cols)
    emission = jnp.where(lev_index == 0, surface, 0.0)
    state = state.at[0].add(emission)
    state = transport(state, coeffs, False)
    state = state.at[0].add(emission)
    slots = sound_col.shape[0]
    live = lax.iota(jnp.int32, slots) < sound_count[0]
    chooser = (sound_prof[:, None] == lax.iota(jnp.int32, profiles.shape[0])[None, :]).astype(
        jnp.float32
    )
    weights = jnp.dot(chooser, profiles, precision=highest, preferred_element_type=jnp.float32)
    flat = state.reshape(levels, rows * cols)
    values = jnp.take(flat, sound_col, axis=1)
    partial_column = jnp.sum(weights * values.T, axis=1)
    column = lax.psum(partial_column, "lev")
    modeled = jnp.where(live, column, 0.0)
    scaled = (column - sound_obs) / sound_sigma
    size_abs = jnp.abs(scaled)
    huber = jnp.where(size_abs <= 1.0, 0.5 * scaled * scaled, size_abs - 0.5)
    misfit = jnp.where(live, huber, 0.0)
    slope = jnp.where(live, jnp.clip(scaled, -1.0, 1.0) / sound_sigma, 0.0)
    adjoint_two = (
        jnp.zeros((levels, rows * cols), jnp.float32)
        .at[:, sound_col]
        .add((weights * slope[:, None]).T)
    )
    adjoint_two = adjoint_two.reshape(levels, rows, cols)
    adjoint_one = transport(adjoint_two, coeffs, True)
    surface_bar = (adjoint_two[0] + adjoint_one[0]).reshape(blocks, block_size)
    shared = spread(surface_bar, "lev", 0)
    piece = lax.all_gather(shared, "tile", axis=0, tiled=True)
    local = global_rows
    inside = (local >= 0) & (local < piece.shape[0])
    found = piece[jnp.clip(local, 0, piece.shape[0] - 1)]
    picked = jnp.where(inside[:, None], found, 0.0)
    state_gradient = transport(adjoint_one, coeffs, True)
    per_entry = jnp.einsum(
        "ecf,ec->ef", remap_weights, picked, precision=highest, preferred_element_type=jnp.float32
    )
    flux_gradient = per_entry.reshape(-1, 2, flux_cells).sum(axis=1)
    return (modeled, misfit, state_gradient, flux_gradient)


def solution(mesh):
    in_specs = (
        P("lev", "tile", None),
        P("lev", "tile", None),
        P("lev", "tile", None),
        P("lev", "tile", None),
        P(("tile", "lev"), None),
        P(("tile", "lev"), None, None),
        P(("tile", "lev"), None),
        P(("tile", "lev")),
        P(None, "lev"),
        P("tile"),
        P("tile"),
        P("tile"),
        P("tile"),
        P("tile"),
    )
    out_specs = (P("tile"), P("tile"), P("lev", "tile", None), P(("tile", "lev"), None))
    return jax.shard_map(
        on_device, mesh=mesh, in_specs=in_specs, out_specs=out_specs, check_vma=False
    )
```

profile of v0, /device:TPU:1, one launch (start us, length us, event | category | flops | bytes accessed | tf_op | source)
XLA Modules:
  0.0 527.5 jit_solution(2005856209609383764)
XLA Ops:
  8.4 11.2 %fusion.93 = f32[90,1,128]{2,1,0:T(1,128)S(1)} fusion(f32[90,128,128]{2,1,0:T(8,128)} %param.23, f32[90,128,1]{1,2,0:T(1,128)S(1)} %bitcast.55), kind=kOutput, calls=%fused_computation.180 | convolution fusion | flops 17694720 | bytes 5990400 | tf_op jit(solution)/shard_map/ecf,ef->ec/dot_general | solution.py:103
  19.6 3.8 scatter_custom_fusion
  23.3 4.5 slice.304
  29.6 4.6 collective-permute-start.1
  36.9 3.3 collective-permute-start
  41.1 3.5 collective-permute-start.4
  50.1 4.0 collective-permute-start.5
  57.8 76.1 %reduce-scatter.4.cloned.1.call-done = f32[360,128]{1,0:T(8,128)} async-done(((f32[11520,128]{1,0:T(8,128)}), f32[360,128]{1,0:T(8,128)}) %reduce-scatter.4.cloned.1.call-update) | async-done | bytes 184336
  134.9 6.5 %fusion.46 = f32[6,64,720]{2,1,0:T(8,128)S(1)} fusion(f32[6,64,720]{2,1,0:T(8,128)} %param.18, f32[1,66,720]{2,1,0:T(8,128)} %copy-done.30, f32[6,1,720]{2,1,0:T(1,128)} %collective-permute-done.2, f32[6,1,720]{2,1,0:T(1,128)} %collective-permute-done.1, f32[1,66,720]{2,1,0:T(8,128)} %copy-done.29, f32[6,64,719]{2,1,0:T(8,128)} %get-tuple-element.55, ...), kind=kLoop, calls=%fused_computation.76 | loop fusion | flops 12441600 | bytes 11473990 | tf_op jit(solution)/shard_map/add | solution.py:56
  141.4 67.9 %all-reduce.4.cloned.1.call-done = f32[360,128]{1,0:T(8,128)} async-done(((f32[360,128]{1,0:T(8,128)}), f32[360,128]{1,0:T(8,128)}) %all-reduce.4.cloned.1.call-update) | async-done | bytes 184336 | tf_op jit(solution)/shard_map/psum | solution.py:114
  213.7 9.0 %collective-permute-start.6 = (f32[6,1,720]{2,1,0:T(1,128)S(1)}, f32[6,1,720]{2,1,0:T(1,128)S(1)}, u32[]{:S(2)}, u32[]{:S(2)}) collective-permute-start(f32[6,1,720]{2,1,0:T(1,128)S(1)} %get-tuple-element.52), channel_id=1, source_target_pairs={{0,8},{8,16},{16,24},{24,32},{32,40},{40,48},{48,56},{56,64},{64,7... | collective-permute-start | bytes 51848 | tf_op jit(solution)/shard_map/ppermute | solution.py:17
  225.1 2.7 collective-permute-done.7
  229.1 4.0 collective-permute-start.9
  233.2 3.6 collective-permute-done.8
  237.1 3.6 fusion.33
  242.3 11.9 %copy.79 = f32[6,64,720]{0,2,1:T(8,128)} copy(f32[6,64,720]{2,1,0:T(8,128)} %fusion.70) | data formatting | bytes 2211840 | tf_op jit(solution)/shard_map/scatter-add | solution.py:118
  254.3 13.2 %gather_fusion = f32[2048,6]{1,0:T(8,128)S(1)} fusion(f32[6,46080]{0,1:T(8,128)} %bitcast.49, s32[2048]{0:T(1024)S(1)} %get-tuple-element.64), kind=kCustom, calls=%fused_computation | custom fusion | bytes 106496 | tf_op jit(solution)/shard_map/jit(_take)/gather | solution.py:126
  268.8 15.9 %psum.22 = f32[2048]{0:T(1024)S(1)} all-reduce(f32[2048]{0:T(1024)S(1)} %get-tuple-element.67), channel_id=1, replica_groups=mesh['tile'=32,'lev'=8] {'lev'}, use_global_device_ids=true, to_apply=%region_4.5 | all-reduce | flops 2048 | bytes 16384 | tf_op jit(solution)/shard_map/psum | solution.py:128
  285.8 20.8 %scatter_custom_fusion.1 = f32[6,46080]{0,1:T(8,128)} fusion(s32[2048]{0:T(1024)} %get-tuple-element.63, f32[2048,6]{1,0:T(8,128)S(1)} %copy.81, f32[]{:T(128)} %constant.93.clone.1), kind=kCustom, calls=%fused_computation.5 | custom fusion | flops 12288 | bytes 1106432 | tf_op jit(solution)/shard_map/scatter-add | solution.py:138
  306.6 11.9 %slice_reduce_fusion = f32[46080]{0:T(1024)} fusion(f32[6,46080]{0,1:T(8,128)} %scatter_custom_fusion.1), kind=kLoop, calls=%fused_computation.4 | loop fusion | bytes 368640 | tf_op jit(solution)/shard_map/slice | solution.py:142
  318.5 12.5 %copy.88 = f32[6,64,720]{2,1,0:T(8,128)S(1)} copy(f32[6,64,720]{0,2,1:T(8,128)} %bitcast.40) | data formatting | bytes 2211840 | tf_op jit(solution)/shard_map/reshape | solution.py:140
  331.1 7.2 %collective-permute-start.11 = (f32[6,1,720]{2,1,0:T(1,128)S(1)}, f32[6,1,720]{2,1,0:T(1,128)S(1)}, u32[]{:S(2)}, u32[]{:S(2)}) collective-permute-start(f32[6,1,720]{2,1,0:T(1,128)S(1)} %get-tuple-element.46), channel_id=1, source_target_pairs={{0,8},{8,16},{16,24},{24,32},{32,40},{40,48},{48,56},{56,64},{64,7... | collective-permute-start | bytes 51848 | tf_op jit(solution)/shard_map/ppermute | solution.py:17
  344.8 4.0 collective-permute-start.13
  348.9 3.2 collective-permute-done.12
  357.2 78.0 %all-reduce.6.cloned.1.call-done = f32[360,128]{1,0:T(8,128)} async-done(((f32[360,128]{1,0:T(8,128)}), f32[360,128]{1,0:T(8,128)}) %all-reduce.6.cloned.1.call-update) | async-done | bytes 184336 | tf_op jit(solution)/shard_map/psum | solution.py:34
  435.3 9.0 %collective-permute-start.15 = (f32[6,1,720]{2,1,0:T(1,128)S(1)}, f32[6,1,720]{2,1,0:T(1,128)S(1)}, u32[]{:S(2)}, u32[]{:S(2)}) collective-permute-start(f32[6,1,720]{2,1,0:T(1,128)S(1)} %get-tuple-element.40), channel_id=1, source_target_pairs={{0,8},{8,16},{16,24},{24,32},{32,40},{40,48},{48,56},{56,64},{64,7... | collective-permute-start | bytes 51848 | tf_op jit(solution)/shard_map/ppermute | solution.py:17
  450.7 4.2 collective-permute-start.17
  455.1 5.8 %collective-permute-done.16 = f32[1,66,720]{2,1,0:T(8,128)S(1)} collective-permute-done((f32[1,66,720]{2,1,0:T(8,128)S(1)}, f32[1,66,720]{2,1,0:T(8,128)S(1)}, u32[]{:S(2)}, u32[]{:S(2)}) %collective-permute-start.16) | collective-permute-done | bytes 190112 | tf_op jit(solution)/shard_map/ppermute | solution.py:19
  460.9 3.3 fusion.7
  464.2 45.7 %all-gather.2.cloned.1.call-done = f32[11520,128]{1,0:T(8,128)} async-done(((f32[360,128]{1,0:T(8,128)}), f32[11520,128]{1,0:T(8,128)}) %all-gather.2.cloned.1.call-update) | async-done | bytes 5898256 | tf_op jit(solution)/shard_map/all_gather | solution.py:144
  509.9 3.3 gather_fusion.1
  513.3 7.0 %fusion.76 = f32[90,1,128]{2,1,0:T(1,128)S(1)} fusion(f32[90,128,128]{2,1,0:T(8,128)} %param.23, f32[90,128,1]{1,0,2:T(8,128)S(1)} %select_bitcast_fusion), kind=kOutput, calls=%fused_computation.147 | convolution fusion | flops 17694720 | bytes 5990400 | tf_op jit(solution)/shard_map/ecf,ec->ef/dot_general | solution.py:150
  (159 shorter events, 47.0 us)
Async XLA Ops:
  7.2 126.8 %reduce-scatter.4.cloned.1.call-start = ((), (), s32[]{:S(2)}) async-start(), calls=%async_computation.4 | async-start | bytes 6082560
  27.9 181.4 %all-reduce.4.cloned.1.call-start = ((), (), s32[]{:S(2)}) async-start(), calls=%async_computation.1 | async-start | bytes 368640 | tf_op jit(solution)/shard_map/psum | solution.py:114
  29.6 18.2 %collective-permute-start.1 = (f32[6,1,720]{2,1,0:T(1,128)}, f32[6,1,720]{2,1,0:T(1,128)}, u32[]{:S(2)}, u32[]{:S(2)}) collective-permute-start(f32[6,1,720]{2,1,0:T(1,128)} %get-tuple-element.58), channel_id=1, source_target_pairs={{0,8},{8,16},{16,24},{24,32},{32,40},{40,48},{48,56},{56,64},{64,7... | collective-permute-start | bytes 51848 | tf_op jit(solution)/shard_map/ppermute | solution.py:17
  34.2 13.7 %collective-permute-start.2 = (f32[6,1,720]{2,1,0:T(1,128)}, f32[6,1,720]{2,1,0:T(1,128)}, u32[]{:S(2)}, u32[]{:S(2)}) collective-permute-start(f32[6,1,720]{2,1,0:T(1,128)} %get-tuple-element.59), channel_id=1, source_target_pairs={{8,0},{16,8},{24,16},{32,24},{40,32},{48,40},{56,48},{64,56},{72,6... | collective-permute-start | bytes 51848 | tf_op jit(solution)/shard_map/ppermute | solution.py:19
  36.8 200.3 %copy-start.3 = (f32[6,64,720]{2,1,0:T(8,128)}, f32[6,64,720]{2,1,0:T(8,128)S(1)}, u32[]{:S(2)}) copy-start(f32[6,64,720]{2,1,0:T(8,128)S(1)} %broadcast_select_fusion.1) | copy-start | bytes 3317764
  36.9 20.3 %collective-permute-start = (f32[6,720]{1,0:T(8,128)S(1)}, f32[6,720]{1,0:T(8,128)S(1)}, u32[]{:S(2)}, u32[]{:S(2)}) collective-permute-start(f32[6,720]{1,0:T(8,128)S(1)} %bitcast.56), channel_id=1, source_target_pairs={{0,8},{8,16},{16,24},{24,32},{32,40},{40,48},{48,56},{56,64},{64,7... | collective-permute-start | bytes 51848 | tf_op jit(solution)/shard_map/ppermute | solution.py:29
  41.1 92.9 %collective-permute-start.4 = (f32[64,720]{1,0:T(8,128)}, f32[64,720]{1,0:T(8,128)S(1)}, u32[]{:S(2)}, u32[]{:S(2)}) collective-permute-start(f32[64,720]{1,0:T(8,128)} %slice_bitcast_fusion), channel_id=1, source_target_pairs={{0,1},{1,2},{2,3},{3,4},{4,5},{5,6},{6,7},{8,9},{9,10},{10,11},{11... | collective-permute-start | bytes 552968 | tf_op jit(solution)/shard_map/ppermute | solution.py:29
  48.7 85.4 %collective-permute-start.3 = (f32[1,66,720]{2,1,0:T(8,128)S(1)}, f32[1,66,720]{2,1,0:T(8,128)S(1)}, u32[]{:S(2)}, u32[]{:S(2)}) collective-permute-start(f32[1,66,720]{2,1,0:T(8,128)S(1)} %get-tuple-element.34), channel_id=1, source_target_pairs={{1,0},{2,1},{3,2},{4,3},{5,4},{6,5},{7,6},{9,8},{10,9},{11,10},{12... | collective-permute-start | bytes 570248 | tf_op jit(solution)/shard_map/ppermute | solution.py:19
  50.1 84.0 %collective-permute-start.5 = (f32[1,66,720]{2,1,0:T(8,128)S(1)}, f32[1,66,720]{2,1,0:T(8,128)S(1)}, u32[]{:S(2)}, u32[]{:S(2)}) collective-permute-start(f32[1,66,720]{2,1,0:T(8,128)S(1)} %get-tuple-element.35), channel_id=1, source_target_pairs={{0,1},{1,2},{2,3},{3,4},{4,5},{5,6},{6,7},{8,9},{9,10},{10,11},{11... | collective-permute-start | bytes 570248 | tf_op jit(solution)/shard_map/ppermute | solution.py:17
  134.0 301.2 %all-reduce.6.cloned.1.call-start = ((), (), s32[]{:S(2)}) async-start(), calls=%async_computation.2 | async-start | bytes 368640 | tf_op jit(solution)/shard_map/psum | solution.py:34
  213.7 11.4 %collective-permute-start.6 = (f32[6,1,720]{2,1,0:T(1,128)S(1)}, f32[6,1,720]{2,1,0:T(1,128)S(1)}, u32[]{:S(2)}, u32[]{:S(2)}) collective-permute-start(f32[6,1,720]{2,1,0:T(1,128)S(1)} %get-tuple-element.52), channel_id=1, source_target_pairs={{0,8},{8,16},{16,24},{24,32},{32,40},{40,48},{48,56},{56,64},{64,7... | collective-permute-start | bytes 51848 | tf_op jit(solution)/shard_map/ppermute | solution.py:17
  222.7 5.1 collective-permute-start.7
  227.8 9.0 %collective-permute-start.8 = (f32[1,66,720]{2,1,0:T(8,128)S(1)}, f32[1,66,720]{2,1,0:T(8,128)S(1)}, u32[]{:S(2)}, u32[]{:S(2)}) collective-permute-start(f32[1,66,720]{2,1,0:T(8,128)S(1)} %get-tuple-element.32), channel_id=1, source_target_pairs={{1,0},{2,1},{3,2},{4,3},{5,4},{6,5},{7,6},{9,8},{10,9},{11,10},{12... | collective-permute-start | bytes 570248 | tf_op jit(solution)/shard_map/ppermute | solution.py:19
  229.1 8.0 %collective-permute-start.9 = (f32[1,66,720]{2,1,0:T(8,128)S(1)}, f32[1,66,720]{2,1,0:T(8,128)S(1)}, u32[]{:S(2)}, u32[]{:S(2)}) collective-permute-start(f32[1,66,720]{2,1,0:T(8,128)S(1)} %get-tuple-element.33), channel_id=1, source_target_pairs={{0,1},{1,2},{2,3},{3,4},{4,5},{5,6},{6,7},{8,9},{9,10},{10,11},{11... | collective-permute-start | bytes 570248 | tf_op jit(solution)/shard_map/ppermute | solution.py:17
  254.3 30.5 %copy-start.32 = (f32[2048]{0:T(1024)S(1)}, f32[2048]{0:T(1024)}, u32[]{:S(2)}) copy-start(f32[2048]{0:T(1024)} %param.31) | copy-start | bytes 24580
  254.3 30.5 %copy-start.33 = (f32[2048]{0:T(1024)S(1)}, f32[2048]{0:T(1024)}, u32[]{:S(2)}) copy-start(f32[2048]{0:T(1024)} %param.30) | copy-start | bytes 24580
  331.1 9.6 %collective-permute-start.11 = (f32[6,1,720]{2,1,0:T(1,128)S(1)}, f32[6,1,720]{2,1,0:T(1,128)S(1)}, u32[]{:S(2)}, u32[]{:S(2)}) collective-permute-start(f32[6,1,720]{2,1,0:T(1,128)S(1)} %get-tuple-element.46), channel_id=1, source_target_pairs={{0,8},{8,16},{16,24},{24,32},{32,40},{40,48},{48,56},{56,64},{64,7... | collective-permute-start | bytes 51848 | tf_op jit(solution)/shard_map/ppermute | solution.py:17
  338.4 5.1 collective-permute-start.10
  343.5 8.6 %collective-permute-start.12 = (f32[1,66,720]{2,1,0:T(8,128)S(1)}, f32[1,66,720]{2,1,0:T(8,128)S(1)}, u32[]{:S(2)}, u32[]{:S(2)}) collective-permute-start(f32[1,66,720]{2,1,0:T(8,128)S(1)} %get-tuple-element.30), channel_id=1, source_target_pairs={{1,0},{2,1},{3,2},{4,3},{5,4},{6,5},{7,6},{9,8},{10,9},{11,10},{12... | collective-permute-start | bytes 570248 | tf_op jit(solution)/shard_map/ppermute | solution.py:19
  344.8 8.0 %collective-permute-start.13 = (f32[1,66,720]{2,1,0:T(8,128)S(1)}, f32[1,66,720]{2,1,0:T(8,128)S(1)}, u32[]{:S(2)}, u32[]{:S(2)}) collective-permute-start(f32[1,66,720]{2,1,0:T(8,128)S(1)} %get-tuple-element.31), channel_id=1, source_target_pairs={{0,1},{1,2},{2,3},{3,4},{4,5},{5,6},{6,7},{8,9},{9,10},{10,11},{11... | collective-permute-start | bytes 570248 | tf_op jit(solution)/shard_map/ppermute | solution.py:17
  355.3 79.9 %copy-start.35 = (s32[90]{0:T(128)S(1)}, s32[90]{0:T(128)}, u32[]{:S(2)}) copy-start(s32[90]{0:T(128)} %get-tuple-element.65) | copy-start | bytes 1084
  355.3 80.0 %copy-start.36 = (s32[90]{0:T(128)S(1)}, s32[90]{0:T(128)}, u32[]{:S(2)}) copy-start(s32[90]{0:T(128)} %param.25) | copy-start | bytes 1084
  355.3 80.0 %copy-start.37 = (s32[90,1]{0,1:T(1,128)S(1)}, s32[90,1]{0,1:T(1,128)}, u32[]{:S(2)}) copy-start(s32[90,1]{0,1:T(1,128)} %param.24) | copy-start | bytes 1084
  357.2 152.7 %all-gather.2.cloned.1.call-start = ((), (), s32[]{:S(2)}) async-start(), calls=%async_computation.3 | async-start | bytes 6082560 | tf_op jit(solution)/shard_map/all_gather | solution.py:144
  435.3 11.4 %collective-permute-start.15 = (f32[6,1,720]{2,1,0:T(1,128)S(1)}, f32[6,1,720]{2,1,0:T(1,128)S(1)}, u32[]{:S(2)}, u32[]{:S(2)}) collective-permute-start(f32[6,1,720]{2,1,0:T(1,128)S(1)} %get-tuple-element.40), channel_id=1, source_target_pairs={{0,8},{8,16},{16,24},{24,32},{32,40},{40,48},{48,56},{56,64},{64,7... | collective-permute-start | bytes 51848 | tf_op jit(solution)/shard_map/ppermute | solution.py:17
  444.3 5.1 collective-permute-start.14
  446.2 14.6 %copy-start.13 = (f32[6,64,720]{2,1,0:T(8,128)S(1)}, f32[6,64,720]{2,1,0:T(8,128)}, u32[]{:S(2)}) copy-start(f32[6,64,720]{2,1,0:T(8,128)} %param.19) | copy-start | bytes 3317764
  446.3 14.6 %copy-start.16 = (f32[5,64,720]{2,1,0:T(8,128)S(1)}, f32[5,64,720]{2,1,0:T(8,128)}, u32[]{:S(2)}) copy-start(f32[5,64,720]{2,1,0:T(8,128)} %slice.302) | copy-start | bytes 2764804
  446.3 14.6 %copy-start.20 = (f32[6,64,1]{2,1,0:T(8,128)S(1)}, f32[6,64,1]{2,1,0:T(8,128)}, u32[]{:S(2)}) copy-start(f32[6,64,1]{2,1,0:T(8,128)} %slice.242) | copy-start | bytes 4612
  446.3 14.6 %copy-start.24 = (f32[64,720]{1,0:T(8,128)S(1)}, f32[64,720]{1,0:T(8,128)}, u32[]{:S(2)}) copy-start(f32[64,720]{1,0:T(8,128)} %copy-done.21) | copy-start | bytes 552964
  449.4 11.4 %collective-permute-start.16 = (f32[1,66,720]{2,1,0:T(8,128)S(1)}, f32[1,66,720]{2,1,0:T(8,128)S(1)}, u32[]{:S(2)}, u32[]{:S(2)}) collective-permute-start(f32[1,66,720]{2,1,0:T(8,128)S(1)} %get-tuple-element.28), channel_id=1, source_target_pairs={{1,0},{2,1},{3,2},{4,3},{5,4},{6,5},{7,6},{9,8},{10,9},{11,10},{12... | collective-permute-start | bytes 570248 | tf_op jit(solution)/shard_map/ppermute | solution.py:19
  450.7 10.1 %collective-permute-start.17 = (f32[1,66,720]{2,1,0:T(8,128)S(1)}, f32[1,66,720]{2,1,0:T(8,128)S(1)}, u32[]{:S(2)}, u32[]{:S(2)}) collective-permute-start(f32[1,66,720]{2,1,0:T(8,128)S(1)} %get-tuple-element.29), channel_id=1, source_target_pairs={{0,1},{1,2},{2,3},{3,4},{4,5},{5,6},{6,7},{8,9},{9,10},{10,11},{11... | collective-permute-start | bytes 570248 | tf_op jit(solution)/shard_map/ppermute | solution.py:17
  (30 other events, 284.1 us)
Sparse Core Ops, SparseCore 0:
  28.0 105.9 reduce-scatter.3
  136.6 72.6 all-reduce.3
  357.3 77.8 all-reduce.5
  437.7 72.1 all-gather.1
where the time goes:
time: 529 us; the launch traced here: 527 us
  waiting for transfers between devices  289 us (55%)
  local copies, waits for them, and re-layouts  70.2 us (13%)
  starting transfers between devices  66.4 us (13%)
  other arithmetic  51.3 us (10%)
  matrix products  19.1 us (4%)
  blocking collectives  15.9 us (3%)
  between operations  15.3 us (3%)
    psum x1, waiting for transfers between devices, spread(): return lax.psum(block, axis)  78 us
    unnamed x5, waiting for transfers between devices  76.2 us
    psum x1, waiting for transfers between devices, on_device(): surface = lax.psum(partial_value, 'lev').reshape(rows, cols)  67.9 us
    ppermute x8, starting transfers between devices, with_halo(): lax.ppermute(tail, axis, [(i, (i + 1) % count) for i in range(ends)])  46 us
    all_gather x1, waiting for transfers between devices, on_device(): piece = lax.all_gather(shared, 'tile', axis=0, tiled=True)  45.7 us
    scatter-add x1, other arithmetic, on_device(): adjoint_two = jnp.zeros((levels, rows * cols), jnp.float32).at[:, sound_c...  20.8 us
    ppermute x8, waiting for transfers between devices, with_halo(): lax.ppermute(head, axis, [((i + 1) % count, i) for i in range(ends)])  20.6 us
    psum x1, blocking collectives, on_device(): column = lax.psum(partial_column, 'lev')  15.9 us
  transfers between devices with their start and end apart: 22, of which 12 were waited for; matrix products, arithmetic and copies ran while one was open for 4% of the time, Pallas kernels for 0%

commit v1 on v0

--- a/solution.py
+++ b/solution.py
@@ -141,7 +141,9 @@
     adjoint_one = transport(adjoint_two, coeffs, True)
     surface_bar = (adjoint_two[0] + adjoint_one[0]).reshape(blocks, block_size)
     shared = spread(surface_bar, "lev", 0)
-    piece = lax.all_gather(shared, "tile", axis=0, tiled=True)
+    piece = jnp.concatenate(
+        lax.all_to_all(jnp.stack([shared] * lax.axis_size("tile")), "tile", 0, 0), axis=0
+    )
     local = global_rows
     inside = (local >= 0) & (local < piece.shape[0])
     found = piece[jnp.clip(local, 0, piece.shape[0] - 1)]

time: 529 us -> 652 us (1.23)
  the two profiles are of different devices: /device:TPU:1 before, /device:TPU:66 now
where the time goes in v1:
time: 652 us; the launch traced here: 643 us
  waiting for transfers between devices  358 us (55%)
  local copies, waits for them, and re-layouts  96.3 us (15%)
  starting transfers between devices  71.9 us (11%)
  other arithmetic  67.5 us (10%)
  matrix products  19.1 us (3%)
  between operations  15.6 us (2%)
  blocking collectives  14.2 us (2%)
    ppermute x8, waiting for transfers between devices, with_halo(): lax.ppermute(tail, axis, [(i, (i + 1) % count) for i in range(ends)])  137 us
    psum x1, waiting for transfers between devices, spread(): return lax.psum(block, axis)  75.9 us
    unnamed x4, waiting for transfers between devices  68.1 us
    psum x1, waiting for transfers between devices, on_device(): surface = lax.psum(partial_value, 'lev').reshape(rows, cols)  67.8 us
    ppermute x8, starting transfers between devices, with_halo(): lax.ppermute(head, axis, [((i + 1) % count, i) for i in range(ends)])  36.1 us
    add x4, other arithmetic, apply_step(): return field + rows_term + cols_term + diffusion  32.7 us
    scatter-add x3, local copies, waits for them, and re-layouts, on_device(): state = state.at[0].add(emission)  23.5 us
    scatter-add x1, other arithmetic, on_device(): adjoint_two = jnp.zeros((levels, rows * cols), jnp.float32).at[:, sound_c...  20.7 us
  transfers between devices with their start and end apart: 22, of which 12 were waited for; matrix products, arithmetic and copies ran while one was open for 6% of the time, Pallas kernels for 0%

profile of v1, /device:TPU:66, one launch (start us, length us, event | category | flops | bytes accessed | tf_op | source)
XLA Modules:
  0.0 643.0 jit_solution(6239250808441660258)
XLA Ops:
  7.9 11.2 %fusion.92 = f32[90,1,128]{2,1,0:T(1,128)S(1)} fusion(f32[90,128,128]{2,1,0:T(8,128)} %param.23, f32[90,128,1]{1,2,0:T(1,128)S(1)} %bitcast.53), kind=kOutput, calls=%fused_computation.176 | convolution fusion | flops 17694720 | bytes 5990400 | tf_op jit(solution)/shard_map/ecf,ef->ec/dot_general | solution.py:103
  19.1 3.8 scatter_custom_fusion
  22.9 4.5 slice.314
  42.3 3.8 collective-permute-start.4
  64.1 68.1 %reduce-scatter.4.cloned.1.call-done = f32[360,128]{1,0:T(8,128)} async-done(((f32[11520,128]{1,0:T(8,128)}), f32[360,128]{1,0:T(8,128)}) %reduce-scatter.4.cloned.1.call-update) | async-done | bytes 184336
  132.7 10.5 %fusion.46 = f32[6,64,720]{2,0,1:T(8,128)S(1)} fusion(f32[6,64,720]{2,0,1:T(8,128)} %copy-done.15, f32[6,66,720]{2,0,1:T(8,128)} %copy-done.30, f32[1,66,720]{2,0,1:T(1,128)} %collective-permute-done.5, f32[1,66,720]{2,0,1:T(1,128)} %collective-permute-done.3, f32[6,1,720]{2,0,1:T(8,128)S(1)} %collective-permute-done.2, ...), kind=kLoop, calls=%fused_computation.76 | loop fusion | flops 11335680 | bytes 12614470 | tf_op jit(solution)/shard_map/add | solution.py:56
  143.2 67.8 %all-reduce.4.cloned.1.call-done = f32[360,128]{1,0:T(8,128)} async-done(((f32[360,128]{1,0:T(8,128)}), f32[360,128]{1,0:T(8,128)}) %all-reduce.4.cloned.1.call-update) | async-done | bytes 184336 | tf_op jit(solution)/shard_map/psum | solution.py:114
  215.6 6.5 %scatter-add.25 = f32[6,64,720]{2,0,1:T(8,128)S(1)} dynamic-update-slice(f32[6,64,720]{2,0,1:T(8,128)S(1)} %fusion.46, f32[1,64,720]{2,0,1:T(1,128)} %slice_add_fusion.1, s32[]{:T(128)} %constant.86.clone.1, s32[]{:T(128)} %constant.86.clone.1, s32[]{:T(128)} %constant.86.clone.1) | dynamic-update-slice | bytes 368644 | tf_op jit(solution)/shard_map/scatter-add | solution.py:116
  224.0 6.7 %collective-permute-start.7 = (f32[6,1,720]{2,0,1:T(8,128)S(1)}, f32[6,1,720]{2,0,1:T(8,128)S(1)}, u32[]{:S(2)}, u32[]{:S(2)}) collective-permute-start(f32[6,1,720]{2,0,1:T(8,128)S(1)} %get-tuple-element.65), channel_id=1, source_target_pairs={{8,0},{16,8},{24,16},{32,24},{40,32},{48,40},{56,48},{64,56},{72,6... | collective-permute-start | bytes 51848 | tf_op jit(solution)/shard_map/ppermute | solution.py:19
  235.0 3.5 collective-permute-start.9
  238.6 3.7 collective-permute-done.8
  242.4 4.5 collective-permute-done.9
  247.0 7.5 %fusion.33 = f32[6,64,720]{2,0,1:T(8,128)S(1)} fusion(f32[6,64,720]{2,0,1:T(8,128)S(1)} %scatter-add.25, f32[1,66,720]{2,0,1:T(1,128)S(1)} %collective-permute-done.9, f32[6,1,720]{2,0,1:T(8,128)S(1)} %collective-permute-done.7, f32[6,1,720]{2,0,1:T(8,128)S(1)} %collective-permute-done.6, f32[1,66,720]{2,0,1:T(1,128)S(1)} %collective-permute-done.8, ...), kind=kLoop, calls=%fused_computation.55 | loop fusion | flops 12441600 | bytes 11473990 | tf_op jit(solution)/shard_map/add | solution.py:56
  255.8 5.0 scatter-add.26
  260.8 12.0 %copy.147 = f32[6,64,720]{0,2,1:T(8,128)} copy(f32[6,64,720]{2,0,1:T(8,128)} %scatter-add.26) | data formatting | bytes 2211840 | tf_op jit(solution)/shard_map/scatter-add | solution.py:118
  272.8 13.2 %gather_fusion = f32[2048,6]{1,0:T(8,128)S(1)} fusion(f32[6,46080]{0,1:T(8,128)} %bitcast.47, s32[2048]{0:T(1024)S(1)} %get-tuple-element.76), kind=kCustom, calls=%fused_computation | custom fusion | bytes 106496 | tf_op jit(solution)/shard_map/jit(_take)/gather | solution.py:126
  287.4 14.2 %psum.22 = f32[2048]{0:T(1024)S(1)} all-reduce(f32[2048]{0:T(1024)S(1)} %get-tuple-element.79), channel_id=1, replica_groups=mesh['tile'=32,'lev'=8] {'lev'}, use_global_device_ids=true, to_apply=%region_4.5 | all-reduce | flops 2048 | bytes 16384 | tf_op jit(solution)/shard_map/psum | solution.py:128
  302.7 20.7 %scatter_custom_fusion.1 = f32[6,46080]{0,1:T(8,128)} fusion(s32[2048]{0:T(1024)S(1)} %get-tuple-element.75, f32[2048,6]{1,0:T(8,128)S(1)} %copy.149, f32[]{:T(128)} %constant.93.clone.1), kind=kCustom, calls=%fused_computation.5 | custom fusion | flops 12288 | bytes 1105924 | tf_op jit(solution)/shard_map/scatter-add | solution.py:138
  323.4 11.9 %slice_reduce_fusion = f32[46080]{0:T(1024)} fusion(f32[6,46080]{0,1:T(8,128)} %scatter_custom_fusion.1), kind=kLoop, calls=%fused_computation.4 | loop fusion | bytes 368640 | tf_op jit(solution)/shard_map/slice | solution.py:142
  335.3 12.5 %copy.156 = f32[6,64,720]{2,0,1:T(8,128)S(1)} copy(f32[6,64,720]{0,2,1:T(8,128)} %bitcast.41) | data formatting | bytes 2211840 | tf_op jit(solution)/shard_map/reshape | solution.py:140
  349.8 6.7 %collective-permute-start.10 = (f32[6,1,720]{2,0,1:T(8,128)S(1)}, f32[6,1,720]{2,0,1:T(8,128)S(1)}, u32[]{:S(2)}, u32[]{:S(2)}) collective-permute-start(f32[6,1,720]{2,0,1:T(8,128)S(1)} %get-tuple-element.59), channel_id=1, source_target_pairs={{8,0},{16,8},{24,16},{32,24},{40,32},{48,40},{56,48},{64,56},{72,6... | collective-permute-start | bytes 51848 | tf_op jit(solution)/shard_map/ppermute | solution.py:19
  358.2 5.2 collective-permute-start.12
  367.5 5.0 collective-permute-done.13
  372.6 7.3 %fusion.20 = f32[6,64,720]{2,0,1:T(8,128)S(1)} fusion(f32[6,64,720]{2,0,1:T(8,128)S(1)} %copy.156, f32[1,66,720]{2,0,1:T(1,128)S(1)} %collective-permute-done.13, f32[6,1,720]{2,0,1:T(8,128)S(1)} %collective-permute-done.10, f32[6,1,720]{2,0,1:T(8,128)S(1)} %collective-permute-done.11, f32[1,66,720]{2,0,1:T(1,128)S(1)} %collective-permute-done.12, ...), kind=kLoop, calls=%fused_computation.34 | loop fusion | flops 10229760 | bytes 11473990 | tf_op jit(solution)/shard_map/add | solution.py:56
  382.3 75.9 %all-reduce.6.cloned.1.call-done = f32[360,128]{1,0:T(8,128)} async-done(((f32[360,128]{1,0:T(8,128)}), f32[360,128]{1,0:T(8,128)}) %all-reduce.6.cloned.1.call-update) | async-done | bytes 184336 | tf_op jit(solution)/shard_map/psum | solution.py:34
  458.2 3.8 stack.2
  462.0 9.3 %all-to-all-start = ((f32[32,360,128]{2,1,0:T(8,128)}), f32[32,360,128]{2,1,0:T(8,128)}, u32[]{:S(2)}, u32[]{:S(2)}) async-start(f32[32,360,128]{2,1,0:T(8,128)} %stack.2), calls=%async_computation | async-start | bytes 11796480 | tf_op jit(solution)/shard_map/all_to_all | solution.py:145
  473.4 6.8 %collective-permute-start.14 = (f32[6,1,720]{2,0,1:T(8,128)S(1)}, f32[6,1,720]{2,0,1:T(8,128)S(1)}, u32[]{:S(2)}, u32[]{:S(2)}) collective-permute-start(f32[6,1,720]{2,0,1:T(8,128)S(1)} %get-tuple-element.53), channel_id=1, source_target_pairs={{8,0},{16,8},{24,16},{32,24},{40,32},{48,40},{56,48},{64,56},{72,6... | collective-permute-start | bytes 51848 | tf_op jit(solution)/shard_map/ppermute | solution.py:19
  480.8 124.8 %collective-permute-done.15 = f32[6,1,720]{2,0,1:T(8,128)S(1)} collective-permute-done((f32[6,1,720]{2,0,1:T(8,128)S(1)}, f32[6,1,720]{2,0,1:T(8,128)S(1)}, u32[]{:S(2)}, u32[]{:S(2)}) %collective-permute-start.15) | collective-permute-done | bytes 17312 | tf_op jit(solution)/shard_map/ppermute | solution.py:17
  607.9 3.9 collective-permute-start.17
  616.5 7.3 %fusion.7 = f32[6,64,720]{2,0,1:T(8,128)S(1)} fusion(f32[6,64,720]{2,0,1:T(8,128)S(1)} %fusion.20, f32[1,66,720]{2,0,1:T(1,128)S(1)} %collective-permute-done.17, f32[6,1,720]{2,0,1:T(8,128)S(1)} %collective-permute-done.14, f32[6,1,720]{2,0,1:T(8,128)S(1)} %collective-permute-done.15, f32[1,66,720]{2,0,1:T(1,128)S(1)} %collective-permute-done.16, ...), kind=kLoop, calls=%fused_computation.13 | loop fusion | flops 10229760 | bytes 11473990 | tf_op jit(solution)/shard_map/add | solution.py:56
  628.6 7.0 %fusion.74 = f32[90,1,128]{2,1,0:T(1,128)S(1)} fusion(f32[90,128,128]{2,1,0:T(8,128)} %param.23, f32[90,128,1]{1,0,2:T(8,128)S(1)} %select_bitcast_fusion), kind=kOutput, calls=%fused_computation.140 | convolution fusion | flops 17694720 | bytes 5990400 | tf_op jit(solution)/shard_map/ecf,ec->ef/dot_general | solution.py:152
  (166 shorter events, 72.7 us)
Async XLA Ops:
  7.2 125.0 %reduce-scatter.4.cloned.1.call-start = ((), (), s32[]{:S(2)}) async-start(), calls=%async_computation.4 | async-start | bytes 6082560
  27.4 183.7 %all-reduce.4.cloned.1.call-start = ((), (), s32[]{:S(2)}) async-start(), calls=%async_computation.2 | async-start | bytes 368640 | tf_op jit(solution)/shard_map/psum | solution.py:114
  29.5 20.4 %collective-permute-start.2 = (f32[6,1,720]{2,0,1:T(8,128)S(1)}, f32[6,1,720]{2,0,1:T(8,128)S(1)}, u32[]{:S(2)}, u32[]{:S(2)}) collective-permute-start(f32[6,1,720]{2,0,1:T(8,128)S(1)} %get-tuple-element.70), channel_id=1, source_target_pairs={{8,0},{16,8},{24,16},{32,24},{40,32},{48,40},{56,48},{64,56},{72,6... | collective-permute-start | bytes 51848 | tf_op jit(solution)/shard_map/ppermute | solution.py:19
  33.0 16.2 %collective-permute-start.1 = (f32[6,1,720]{2,0,1:T(8,128)S(1)}, f32[6,1,720]{2,0,1:T(8,128)S(1)}, u32[]{:S(2)}, u32[]{:S(2)}) collective-permute-start(f32[6,1,720]{2,0,1:T(8,128)S(1)} %get-tuple-element.71), channel_id=1, source_target_pairs={{0,8},{8,16},{16,24},{24,32},{32,40},{40,48},{48,56},{56,64},{64,7... | collective-permute-start | bytes 51848 | tf_op jit(solution)/shard_map/ppermute | solution.py:17
  36.9 95.8 %collective-permute-start = (f32[6,720]{1,0:T(8,128)S(1)}, f32[6,720]{1,0:T(8,128)S(1)}, u32[]{:S(2)}, u32[]{:S(2)}) collective-permute-start(f32[6,720]{1,0:T(8,128)S(1)} %slice_bitcast_fusion), channel_id=1, source_target_pairs={{0,8},{8,16},{16,24},{24,32},{32,40},{40,48},{48,56},{56,64},{64,7... | collective-permute-start | bytes 51848 | tf_op jit(solution)/shard_map/ppermute | solution.py:29
  41.1 205.8 %copy-start.2 = (f32[6,64,720]{2,0,1:T(8,128)}, f32[6,64,720]{2,0,1:T(8,128)S(1)}, u32[]{:S(2)}) copy-start(f32[6,64,720]{2,0,1:T(8,128)S(1)} %copy_select_fusion) | copy-start | bytes 3317764
  42.3 20.1 %collective-permute-start.4 = (f32[64,720]{1,0:T(8,128)}, f32[64,720]{1,0:T(8,128)}, u32[]{:S(2)}, u32[]{:S(2)}) collective-permute-start(f32[64,720]{1,0:T(8,128)} %bitcast.36), channel_id=1, source_target_pairs={{0,1},{1,2},{2,3},{3,4},{4,5},{5,6},{6,7},{8,9},{9,10},{10,11},{11... | collective-permute-start | bytes 552968 | tf_op jit(solution)/shard_map/ppermute | solution.py:29
  52.2 80.5 %collective-permute-start.3 = (f32[1,66,720]{2,0,1:T(1,128)}, f32[1,66,720]{2,0,1:T(1,128)}, u32[]{:S(2)}, u32[]{:S(2)}) collective-permute-start(f32[1,66,720]{2,0,1:T(1,128)} %get-tuple-element.46), channel_id=1, source_target_pairs={{1,0},{2,1},{3,2},{4,3},{5,4},{6,5},{7,6},{9,8},{10,9},{11,10},{12... | collective-permute-start | bytes 570248 | tf_op jit(solution)/shard_map/ppermute | solution.py:19
  55.2 77.5 %collective-permute-start.5 = (f32[1,66,720]{2,0,1:T(1,128)}, f32[1,66,720]{2,0,1:T(1,128)}, u32[]{:S(2)}, u32[]{:S(2)}) collective-permute-start(f32[1,66,720]{2,0,1:T(1,128)} %get-tuple-element.47), channel_id=1, source_target_pairs={{0,1},{1,2},{2,3},{3,4},{4,5},{5,6},{6,7},{8,9},{9,10},{10,11},{11... | collective-permute-start | bytes 570248 | tf_op jit(solution)/shard_map/ppermute | solution.py:17
  132.2 326.0 %all-reduce.6.cloned.1.call-start = ((), (), s32[]{:S(2)}) async-start(), calls=%async_computation.3 | async-start | bytes 368640 | tf_op jit(solution)/shard_map/psum | solution.py:34
  222.1 9.2 %collective-permute-start.6 = (f32[6,1,720]{2,0,1:T(8,128)S(1)}, f32[6,1,720]{2,0,1:T(8,128)S(1)}, u32[]{:S(2)}, u32[]{:S(2)}) collective-permute-start(f32[6,1,720]{2,0,1:T(8,128)S(1)} %get-tuple-element.64), channel_id=1, source_target_pairs={{0,8},{8,16},{16,24},{24,32},{32,40},{40,48},{48,56},{56,64},{64,7... | collective-permute-start | bytes 51848 | tf_op jit(solution)/shard_map/ppermute | solution.py:17
  224.0 8.2 %collective-permute-start.7 = (f32[6,1,720]{2,0,1:T(8,128)S(1)}, f32[6,1,720]{2,0,1:T(8,128)S(1)}, u32[]{:S(2)}, u32[]{:S(2)}) collective-permute-start(f32[6,1,720]{2,0,1:T(8,128)S(1)} %get-tuple-element.65), channel_id=1, source_target_pairs={{8,0},{16,8},{24,16},{32,24},{40,32},{48,40},{56,48},{64,56},{72,6... | collective-permute-start | bytes 51848 | tf_op jit(solution)/shard_map/ppermute | solution.py:19
  232.5 9.8 %collective-permute-start.8 = (f32[1,66,720]{2,0,1:T(1,128)S(1)}, f32[1,66,720]{2,0,1:T(1,128)S(1)}, u32[]{:S(2)}, u32[]{:S(2)}) collective-permute-start(f32[1,66,720]{2,0,1:T(1,128)S(1)} %get-tuple-element.44), channel_id=1, source_target_pairs={{1,0},{2,1},{3,2},{4,3},{5,4},{6,5},{7,6},{9,8},{10,9},{11,10},{12... | collective-permute-start | bytes 570248 | tf_op jit(solution)/shard_map/ppermute | solution.py:19
  235.0 11.9 %collective-permute-start.9 = (f32[1,66,720]{2,0,1:T(1,128)S(1)}, f32[1,66,720]{2,0,1:T(1,128)S(1)}, u32[]{:S(2)}, u32[]{:S(2)}) collective-permute-start(f32[1,66,720]{2,0,1:T(1,128)S(1)} %get-tuple-element.45), channel_id=1, source_target_pairs={{0,1},{1,2},{2,3},{3,4},{4,5},{5,6},{6,7},{8,9},{9,10},{10,11},{11... | collective-permute-start | bytes 570248 | tf_op jit(solution)/shard_map/ppermute | solution.py:17
  272.8 28.8 %copy-start.33 = (f32[2048]{0:T(1024)S(1)}, f32[2048]{0:T(1024)}, u32[]{:S(2)}) copy-start(f32[2048]{0:T(1024)} %param.31) | copy-start | bytes 24580
  272.8 28.8 %copy-start.34 = (f32[2048]{0:T(1024)S(1)}, f32[2048]{0:T(1024)}, u32[]{:S(2)}) copy-start(f32[2048]{0:T(1024)} %param.30) | copy-start | bytes 24580
  347.8 9.2 %collective-permute-start.11 = (f32[6,1,720]{2,0,1:T(8,128)S(1)}, f32[6,1,720]{2,0,1:T(8,128)S(1)}, u32[]{:S(2)}, u32[]{:S(2)}) collective-permute-start(f32[6,1,720]{2,0,1:T(8,128)S(1)} %get-tuple-element.58), channel_id=1, source_target_pairs={{0,8},{8,16},{16,24},{24,32},{32,40},{40,48},{48,56},{56,64},{64,7... | collective-permute-start | bytes 51848 | tf_op jit(solution)/shard_map/ppermute | solution.py:17
  349.8 8.2 %collective-permute-start.10 = (f32[6,1,720]{2,0,1:T(8,128)S(1)}, f32[6,1,720]{2,0,1:T(8,128)S(1)}, u32[]{:S(2)}, u32[]{:S(2)}) collective-permute-start(f32[6,1,720]{2,0,1:T(8,128)S(1)} %get-tuple-element.59), channel_id=1, source_target_pairs={{8,0},{16,8},{24,16},{32,24},{40,32},{48,40},{56,48},{64,56},{72,6... | collective-permute-start | bytes 51848 | tf_op jit(solution)/shard_map/ppermute | solution.py:19
  358.2 9.3 %collective-permute-start.12 = (f32[1,66,720]{2,0,1:T(1,128)S(1)}, f32[1,66,720]{2,0,1:T(1,128)S(1)}, u32[]{:S(2)}, u32[]{:S(2)}) collective-permute-start(f32[1,66,720]{2,0,1:T(1,128)S(1)} %get-tuple-element.42), channel_id=1, source_target_pairs={{1,0},{2,1},{3,2},{4,3},{5,4},{6,5},{7,6},{9,8},{10,9},{11,10},{12... | collective-permute-start | bytes 570248 | tf_op jit(solution)/shard_map/ppermute | solution.py:19
  363.4 9.1 %collective-permute-start.13 = (f32[1,66,720]{2,0,1:T(1,128)S(1)}, f32[1,66,720]{2,0,1:T(1,128)S(1)}, u32[]{:S(2)}, u32[]{:S(2)}) collective-permute-start(f32[1,66,720]{2,0,1:T(1,128)S(1)} %get-tuple-element.43), channel_id=1, source_target_pairs={{0,1},{1,2},{2,3},{3,4},{4,5},{5,6},{6,7},{8,9},{9,10},{10,11},{11... | collective-permute-start | bytes 570248 | tf_op jit(solution)/shard_map/ppermute | solution.py:17
  462.0 163.1 %all-to-all-start = ((f32[32,360,128]{2,1,0:T(8,128)}), f32[32,360,128]{2,1,0:T(8,128)}, u32[]{:S(2)}, u32[]{:S(2)}) async-start(f32[32,360,128]{2,1,0:T(8,128)} %stack.2), calls=%async_computation | async-start | bytes 11796480 | tf_op jit(solution)/shard_map/all_to_all | solution.py:145
  471.4 134.2 %collective-permute-start.15 = (f32[6,1,720]{2,0,1:T(8,128)S(1)}, f32[6,1,720]{2,0,1:T(8,128)S(1)}, u32[]{:S(2)}, u32[]{:S(2)}) collective-permute-start(f32[6,1,720]{2,0,1:T(8,128)S(1)} %get-tuple-element.52), channel_id=1, source_target_pairs={{0,8},{8,16},{16,24},{24,32},{32,40},{40,48},{48,56},{56,64},{64,7... | collective-permute-start | bytes 51848 | tf_op jit(solution)/shard_map/ppermute | solution.py:17
  473.4 132.2 %collective-permute-start.14 = (f32[6,1,720]{2,0,1:T(8,128)S(1)}, f32[6,1,720]{2,0,1:T(8,128)S(1)}, u32[]{:S(2)}, u32[]{:S(2)}) collective-permute-start(f32[6,1,720]{2,0,1:T(8,128)S(1)} %get-tuple-element.53), channel_id=1, source_target_pairs={{8,0},{16,8},{24,16},{32,24},{40,32},{48,40},{56,48},{64,56},{72,6... | collective-permute-start | bytes 51848 | tf_op jit(solution)/shard_map/ppermute | solution.py:19
  480.2 136.2 %copy-start.7 = (f32[6,64,719]{2,0,1:T(8,128)S(1)}, f32[6,64,719]{2,0,1:T(8,128)}, u32[]{:S(2)}) copy-start(f32[6,64,719]{2,0,1:T(8,128)} %copy.203) | copy-start | bytes 3313156
  480.2 136.2 %copy-start.10 = (f32[6,63,720]{2,0,1:T(8,128)S(1)}, f32[6,63,720]{2,0,1:T(8,128)}, u32[]{:S(2)}) copy-start(f32[6,63,720]{2,0,1:T(8,128)} %slice.300) | copy-start | bytes 3265924
  480.2 136.2 %copy-start.19 = (f32[6,64,720]{2,1,0:T(8,128)S(1)}, f32[6,64,720]{2,1,0:T(8,128)}, u32[]{:S(2)}) copy-start(f32[6,64,720]{2,1,0:T(8,128)} %param.19) | copy-start | bytes 3317764
  480.2 136.2 %copy-start.22 = (f32[6,64,720]{2,1,0:T(8,128)S(1)}, f32[6,64,720]{2,1,0:T(8,128)}, u32[]{:S(2)}) copy-start(f32[6,64,720]{2,1,0:T(8,128)} %param.21) | copy-start | bytes 3317764
  480.7 135.7 %copy-start.4 = (f32[6,64,720]{2,0,1:T(8,128)S(1)}, f32[6,64,720]{2,0,1:T(8,128)}, u32[]{:S(2)}) copy-start(f32[6,64,720]{2,0,1:T(8,128)} %copy-done.2) | copy-start | bytes 3317764
  480.8 135.7 %copy-start.14 = (f32[6,64,720]{2,1,0:T(8,128)S(1)}, f32[6,64,720]{2,1,0:T(8,128)}, u32[]{:S(2)}) copy-start(f32[6,64,720]{2,1,0:T(8,128)} %param.20) | copy-start | bytes 3317764
  480.8 135.7 %copy-start.28 = (f32[1,64,720]{2,0,1:T(1,128)S(1)}, f32[1,64,720]{2,0,1:T(1,128)}, u32[]{:S(2)}) copy-start(f32[1,64,720]{2,0,1:T(1,128)} %broadcast_in_dim.90) | copy-start | bytes 552964
  606.0 7.6 %collective-permute-start.16 = (f32[1,66,720]{2,0,1:T(1,128)S(1)}, f32[1,66,720]{2,0,1:T(1,128)S(1)}, u32[]{:S(2)}, u32[]{:S(2)}) collective-permute-start(f32[1,66,720]{2,0,1:T(1,128)S(1)} %get-tuple-element.40), channel_id=1, source_target_pairs={{1,0},{2,1},{3,2},{4,3},{5,4},{6,5},{7,6},{9,8},{10,9},{11,10},{12... | collective-permute-start | bytes 570248 | tf_op jit(solution)/shard_map/ppermute | solution.py:19
  607.9 8.5 %collective-permute-start.17 = (f32[1,66,720]{2,0,1:T(1,128)S(1)}, f32[1,66,720]{2,0,1:T(1,128)S(1)}, u32[]{:S(2)}, u32[]{:S(2)}) collective-permute-start(f32[1,66,720]{2,0,1:T(1,128)S(1)} %get-tuple-element.41), channel_id=1, source_target_pairs={{0,1},{1,2},{2,3},{3,4},{4,5},{5,6},{6,7},{8,9},{9,10},{10,11},{11... | collective-permute-start | bytes 570248 | tf_op jit(solution)/shard_map/ppermute | solution.py:17
  (29 other events, 319.7 us)
Sparse Core Ops, SparseCore 0:
  27.5 104.6 reduce-scatter.3
  134.8 76.2 all-reduce.3
  382.4 75.7 all-reduce.5
